TPU v7x, 512 devices: a whole 4x8x8 slice. The times are simulated.
512 devices in a mesh: site: 128 (over z, x_hi, y), src: 4 (over x_lo, core).
Axes of the slice: x: 4 (x_hi: 2, x_lo: 2; x = x_hi * 2 + x_lo), y: 8, z: 8, core: 2. Of those that a mesh axis runs over, the one named last changes fastest.
Arguments:
- source: float32 [2, 12, 4, 12, 32768], P(None, None, 'src', None, 'site'), may hold values from -6 to 6
- basis: bfloat16 [2, 12, 128, 32768], P(None, None, None, 'site'), may hold values from -0.078125 to 0.078125
- compressed: bfloat16 [2, 512, 128, 12, 128], P(None, 'src', 'site'), may hold values from -0.0390625 to 0.0390625
- eigenvalues: float32 [512], P('src'), may hold values from 0.01 to 0.1
- links: float32 [2, 4, 3, 3, 32768], P(None, None, None, None, 'site'), may hold values from -2.5 to 2.5
Outputs:
- residual: float32 [2, 12, 4, 12, 32768], P(None, None, 'src', None, 'site')
All inputs are finite; a program needn't handle non-finite values.
Results may differ from a plain program's by a relative error of at most 0.0095.
Values may be sent and summed in bfloat16 or wider, within the bound.
A program may use at most 64 MiB of HBM per device.

v0:
```python
import jax
import jax.numpy as jnp
import numpy as np
from jax import lax
from jax.sharding import PartitionSpec as P

EDGE = 4
LS = 12
NV = 128


FIFTH_MASS = 0.4
WALL_HEIGHT = 1.8


def passed_along(value, axis, steps):
    count = lax.axis_size(axis)
    pairs = [(source, (source + steps) % count) for source in range(count)]
    return lax.ppermute(value, axis, pairs)


def partner(block, axis, stride):
    count = lax.axis_size(axis)
    route = []
    for low in range(count):
        high = low | 1 << stride
        if high != low and high < count:
            route += [(low, high), (high, low)]
    return lax.ppermute(block, axis, route)


def times_i(values):
    return jnp.stack([-values[1], values[0]])


def times_minus_i(values):
    return jnp.stack([values[1], -values[0]])


def spin_e(direction, lower_spins):
    first_spin = lower_spins[:, 0]
    second_spin = lower_spins[:, 1]
    if direction == 0:
        spin_pair = (times_i(second_spin), times_i(first_spin))
    elif direction == 1:
        spin_pair = (second_spin, -first_spin)
    elif direction == 2:
        spin_pair = (times_i(first_spin), -times_i(second_spin))
    else:
        spin_pair = (first_spin, second_spin)
    return jnp.stack(spin_pair, axis=1)


def spin_e_dagger(direction, upper_spins):
    first_spin = upper_spins[:, 0]
    second_spin = upper_spins[:, 1]
    if direction == 0:
        spin_pair = (times_minus_i(second_spin), times_minus_i(first_spin))
    elif direction == 1:
        spin_pair = (-second_spin, first_spin)
    elif direction == 2:
        spin_pair = (times_minus_i(first_spin), times_i(second_spin))
    else:
        spin_pair = (first_spin, second_spin)
    return jnp.stack(spin_pair, axis=1)


def colour_times(link_mat, spinor):
    real_terms = []
    imaginary_terms = []
    for colour in range(3):
        link_real = link_mat[0, :, colour][:, None, :]
        link_imag = link_mat[1, :, colour][:, None, :]
        spin_real = spinor[0, :, colour : colour + 1]
        spin_imag = spinor[1, :, colour : colour + 1]
        real_terms.append(link_real * spin_real - link_imag * spin_imag)
        imaginary_terms.append(link_real * spin_imag + link_imag * spin_real)
    return jnp.stack(
        [
            real_terms[0] + real_terms[1] + real_terms[2],
            imaginary_terms[0] + imaginary_terms[1] + imaginary_terms[2],
        ]
    )


def colour_dagger(link_mat, spinor):
    real_terms = []
    imaginary_terms = []
    for colour in range(3):
        link_real = link_mat[0, colour][:, None, :]
        link_imag = link_mat[1, colour][:, None, :]
        spin_real = spinor[0, :, colour : colour + 1]
        spin_imag = spinor[1, :, colour : colour + 1]
        real_terms.append(link_real * spin_real + link_imag * spin_imag)
        imaginary_terms.append(link_real * spin_imag - link_imag * spin_real)
    return jnp.stack(
        [
            real_terms[0] + real_terms[1] + real_terms[2],
            imaginary_terms[0] + imaginary_terms[1] + imaginary_terms[2],
        ]
    )


def site_coord(direction):
    return np.arange(EDGE**4) // EDGE**direction % EDGE


def face_of(field, direction, level):
    stride = EDGE**direction
    every = np.arange(EDGE**3)
    chosen = (every % stride + level * stride + every // stride * (stride * EDGE)).astype(np.int32)
    return jnp.take(field, jnp.asarray(chosen), axis=field.ndim - 1)


def join_face(field, direction, received_values, ahead):
    stride = EDGE**direction
    every = np.arange(EDGE**4)
    slots = (every % stride + every // (stride * EDGE) * stride).astype(np.int32)
    coord = jnp.asarray(site_coord(direction).astype(np.int32))
    expanded = jnp.take(received_values, jnp.asarray(slots), axis=received_values.ndim - 1)
    if ahead:
        return jnp.where(coord == EDGE - 1, expanded, jnp.roll(field, -stride, axis=field.ndim - 1))
    return jnp.where(coord == 0, expanded, jnp.roll(field, stride, axis=field.ndim - 1))


def trade_faces(front, back, direction):
    front_rows = front.shape[0]
    if direction == 3:
        front_incoming = passed_along(front.astype(jnp.bfloat16), "site", -8).astype(front.dtype)
        back_in = passed_along(back.astype(jnp.bfloat16), "site", 8).astype(back.dtype)
        return (front_incoming, back_in)
    packed = jnp.concatenate([front, back], axis=0)
    if direction == 0:
        received = partner(packed, "site", 0)
    elif direction == 1:
        received = partner(packed, "site", 1)
    else:
        received = partner(packed, "site", 2)
    return (received[:front_rows], received[front_rows:])


def both_hops(direction, ahead_half, behind_half, link_mat):
    moved = colour_times(link_mat, ahead_half)
    ahead_full = jnp.concatenate([moved, -spin_e_dagger(direction, moved)], axis=1)
    behind_full = jnp.concatenate([behind_half, spin_e_dagger(direction, behind_half)], axis=1)
    return ahead_full + behind_full


def hop_direction(guess, link_mat, direction):
    cells = EDGE**3
    front = face_of(guess, direction, 0)
    back_guess = face_of(guess, direction, EDGE - 1)
    back_link = face_of(link_mat, direction, EDGE - 1)
    guess_rows = back_guess.size // cells
    back = jnp.concatenate([back_guess.reshape(-1, cells), back_link.reshape(-1, cells)], axis=0)
    front_incoming, back_in = trade_faces(front.reshape(-1, cells), back, direction)
    guess_ahead = join_face(guess, direction, front_incoming.reshape(front.shape), True)
    guess_behind = join_face(
        guess, direction, back_in[:guess_rows].reshape(back_guess.shape), False
    )
    link_behind = join_face(
        link_mat, direction, back_in[guess_rows:].reshape(back_link.shape), False
    )
    ahead_half = guess_ahead[:, 0:2] - spin_e(direction, guess_ahead[:, 2:4])
    behind_sum = guess_behind[:, 0:2] + spin_e(direction, guess_behind[:, 2:4])
    behind_half = colour_dagger(link_behind, behind_sum)
    return both_hops(direction, ahead_half, behind_half, link_mat)


def fifth_terms(guess, src_dev):
    shaped = guess.reshape(guess.shape[:3] + (src_dev, LS, guess.shape[-1]))
    ahead = jnp.concatenate([shaped[:, :, :, :, 1:], -FIFTH_MASS * shaped[:, :, :, :, :1]], axis=4)
    behind = jnp.concatenate(
        [-FIFTH_MASS * shaped[:, :, :, :, -1:], shaped[:, :, :, :, :-1]], axis=4
    )
    return jnp.concatenate([behind[:, 0:2], ahead[:, 2:4]], axis=1).reshape(guess.shape)


def dot_last(left_rows, right_rows):
    return lax.dot_general(
        left_rows, right_rows, (((1,), (1,)), ((), ())), preferred_element_type=jnp.float32
    )


def dot_plain(left_rows, right_rows):
    return jnp.dot(left_rows, right_rows, preferred_element_type=jnp.float32)


def dot_sites(left_rows, right_rows):
    return lax.dot_general(
        left_rows, right_rows, (((0, 2), (0, 2)), ((), ())), preferred_element_type=jnp.float32
    )


def spread_rows(incoming_coarse_rows, basis_portion):
    return jnp.einsum(
        "gc,fcz->fgz", incoming_coarse_rows, basis_portion, preferred_element_type=jnp.float32
    )


def body(source, basis, compressed, eigenvalues, links):
    src_dev = source.shape[2]
    volume = source.shape[4]
    row_count = src_dev * LS
    low_source = source.astype(jnp.bfloat16).reshape(2, 12, row_count, volume)
    proj_real = dot_sites(low_source[0], basis[0]) + dot_sites(low_source[1], basis[1])
    proj_imag = dot_sites(low_source[1], basis[0]) - dot_sites(low_source[0], basis[1])
    low_proj = jnp.stack([proj_real, proj_imag]).astype(jnp.bfloat16).reshape(2, src_dev, LS * NV)
    coarse_table = compressed.reshape(2, compressed.shape[1], LS * NV)
    piece_rows = lax.all_gather(low_proj, "src", axis=1, tiled=True)
    amp_real = dot_last(piece_rows[0], coarse_table[0]) + dot_last(piece_rows[1], coarse_table[1])
    amp_imag = dot_last(piece_rows[1], coarse_table[0]) - dot_last(piece_rows[0], coarse_table[1])
    partial_amplitude = jnp.stack([amp_real, amp_imag])
    amplitudes = lax.psum(partial_amplitude, "site")
    weights = (amplitudes / eigenvalues).astype(jnp.bfloat16)
    coarse_real = dot_plain(weights[0], coarse_table[0]) - dot_plain(weights[1], coarse_table[1])
    coarse_imag = dot_plain(weights[0], coarse_table[1]) + dot_plain(weights[1], coarse_table[0])
    coarse = lax.psum_scatter(
        jnp.stack([coarse_real, coarse_imag], axis=1), "src", scatter_dimension=0, tiled=True
    )
    low_coarse = jnp.transpose(coarse, (1, 0, 2)).astype(jnp.bfloat16).reshape(2, row_count, NV)
    guess_real = spread_rows(low_coarse[0], basis[0]) - spread_rows(low_coarse[1], basis[1])
    guess_imag = spread_rows(low_coarse[0], basis[1]) + spread_rows(low_coarse[1], basis[0])
    guess = jnp.stack([guess_real, guess_imag]).reshape(2, 4, 3, row_count, volume)
    hopping = hop_direction(guess, links[:, 0], 0)
    for direction in range(1, 4):
        hopping = hopping + hop_direction(guess, links[:, direction], direction)
    applied = (5.0 - WALL_HEIGHT) * guess - 0.5 * hopping - fifth_terms(guess, src_dev)
    return source - applied.reshape(source.shape)


def solution(mesh):
    in_specs = (
        P(None, None, "src", None, "site"),
        P(None, None, None, "site"),
        P(None, "src", "site", None, None),
        P("src"),
        P(None, None, None, None, "site"),
    )
    out_specs = P(None, None, "src", None, "site")
    return jax.shard_map(body, mesh=mesh, in_specs=in_specs, out_specs=out_specs, check_vma=False)
```

profile of v0, /device:TPU:1, one launch (start us, length us, event | category | flops | bytes accessed | tf_op | source)
XLA Modules:
  0.0 676.5 jit_solution(17368546450291816944)
XLA Ops:
  5.9 11.9 %all_gather.3 = bf16[2,4,1536]{2,0,1:T(2,128)(2,1)S(1)} all-gather(bf16[2,1,1536]{2,0,1:T(2,128)(2,1)S(1)} %pad_maximum_fusion.12), channel_id=1, replica_groups=mesh['site'=128,'src'=4] {'src'}, dimensions={1}, use_global_device_ids=true | all-gather | bytes 30720 | tf_op jit(solution)/shard_map/all_gather | solution.py:210
  22.6 305.3 %psum.7 = f32[2,4,128]{2,1,0:T(4,128)S(1)} all-reduce(f32[2,4,128]{2,1,0:T(4,128)S(1)} %pad_maximum_fusion.13), channel_id=1, replica_groups=mesh['site'=128,'src'=4] {'site'}, use_global_device_ids=true, to_apply=%region_0.0 | all-reduce | flops 1024 | bytes 8192 | tf_op jit(solution)/shard_map/psum | solution.py:214
  328.8 65.2 %all-reduce = bf16[4,2,1536]{2,1,0:T(2,128)(2,1)S(1)} all-reduce(f32[4,2,1536]{2,1,0:T(2,128)S(1)} %copy.1176), channel_id=2, replica_groups=mesh['site'=128,'src'=4] {'src'}, use_global_device_ids=true, to_apply=%region_1.0.clone | all-reduce | flops 12288 | bytes 73728
  407.4 2.4 gather_fusion.21
  418.2 7.1 %collective-permute-start.3 = (bf16[288,64]{1,0:T(8,128)(2,1)}, bf16[288,64]{1,0:T(8,128)(2,1)}, u32[]{:S(2)}, u32[]{:S(2)}) collective-permute-start(bf16[288,64]{1,0:T(8,128)(2,1)} %convert_element_type.41), channel_id=1, source_target_pairs={{0,480},{4,484},{8,488},{12,492},{16,496},{20,500},{24,504},{28,50... | collective-permute-start | bytes 110600 | tf_op jit(solution)/shard_map/ppermute | solution.py:19
  440.4 2.6 gather_fusion.14
  460.4 2.6 gather_fusion.8
  465.8 11.7 %collective-permute-start.1 = (f32[594,64]{1,0:T(8,128)}, f32[594,64]{1,0:T(8,128)}, u32[]{:S(2)}, u32[]{:S(2)}) collective-permute-start(f32[594,64]{1,0:T(8,128)} %pad_maximum_fusion.2), channel_id=1, source_target_pairs={{0,8},{8,0},{4,12},{12,4},{16,24},{24,16},{20,28},{28,20},{32,40},... | collective-permute-start | bytes 456200 | tf_op jit(solution)/shard_map/ppermute | solution.py:29
  479.6 2.3 select_bitcast_fusion
  521.9 2.2 copy.1286
  524.1 5.7 gather_fusion.19
  529.7 3.8 copy.1287
  539.5 2.2 copy.1303
  541.6 5.7 gather_fusion.23
  547.3 3.8 copy.1304
  554.6 2.6 gather_fusion.22
  557.2 2.3 bitcast_select_fusion
  570.5 2.1 copy.1267
  572.6 5.8 gather_fusion.17
  578.4 3.8 copy.1268
  588.6 2.6 gather_fusion.16
  599.5 4.5 gather_fusion.15
  604.0 3.6 copy.1255
  612.1 4.5 gather_fusion.9
  616.6 3.8 copy.1224
  620.9 4.5 gather_fusion.11
  625.4 3.9 copy.1235
  633.3 2.8 gather_fusion.10
  646.6 4.7 gather_fusion.5
  651.3 3.1 copy.1201
  664.8 4.7 gather_fusion.3
  669.6 3.2 copy.1187
  (538 shorter events, 177.1 us)
Async XLA Ops:
  0.0 18.4 %copy-start.24 = (bf16[2,128,1,12,128]{4,1,3,2,0:T(8,128)(2,1)S(1)}, bf16[2,128,1,12,128]{4,1,3,2,0:T(8,128)(2,1)}, u32[]{:S(2)}) copy-start(bf16[2,128,1,12,128]{4,1,3,2,0:T(8,128)(2,1)} %param.51) | copy-start | bytes 2359300
  5.5 322.4 %copy-start.99 = (f32[128]{0:T(128)S(1)}, f32[128]{0:T(128)}, u32[]{:S(2)}) copy-start(f32[128]{0:T(128)} %param.52) | copy-start | bytes 1540
  397.8 27.6 %copy-start.90 = (s32[256]{0:T(256)S(1)}, s32[256]{0:T(256)}, u32[]{:S(2)}) copy-start(s32[256]{0:T(256)} %constant.308) | copy-start | bytes 3076
  399.1 33.2 %copy-start.89 = (s32[256]{0:T(256)S(1)}, s32[256]{0:T(256)}, u32[]{:S(2)}) copy-start(s32[256]{0:T(256)} %constant.320) | copy-start | bytes 3076
  412.4 123.9 %collective-permute-start.4 = (bf16[306,64]{1,0:T(8,128)(2,1)}, bf16[306,64]{1,0:T(8,128)(2,1)}, u32[]{:S(2)}, u32[]{:S(2)}) collective-permute-start(bf16[306,64]{1,0:T(8,128)(2,1)} %pad_maximum_fusion.5), channel_id=1, source_target_pairs={{0,32},{4,36},{8,40},{12,44},{16,48},{20,52},{24,56},{28,60},{32,6... | collective-permute-start | bytes 117512 | tf_op jit(solution)/shard_map/ppermute | solution.py:19
  414.3 33.4 %copy-start.97 = (s32[64]{0:T(128)S(1)}, s32[64]{0:T(128)}, u32[]{:S(2)}) copy-start(s32[64]{0:T(128)} %constant.311) | copy-start | bytes 772
  418.2 21.0 %copy-start.45 = (f32[2,1,3,3,256]{4,1,3,2,0:T(1,128)S(1)}, f32[2,1,3,3,256]{4,1,3,2,0:T(1,128)}, u32[]{:S(2)}) copy-start(f32[2,1,3,3,256]{4,1,3,2,0:T(1,128)} %get-tuple-element.166) | copy-start | bytes 55300
  418.2 102.1 %collective-permute-start.3 = (bf16[288,64]{1,0:T(8,128)(2,1)}, bf16[288,64]{1,0:T(8,128)(2,1)}, u32[]{:S(2)}, u32[]{:S(2)}) collective-permute-start(bf16[288,64]{1,0:T(8,128)(2,1)} %convert_element_type.41), channel_id=1, source_target_pairs={{0,480},{4,484},{8,488},{12,492},{16,496},{20,500},{24,504},{28,50... | collective-permute-start | bytes 110600 | tf_op jit(solution)/shard_map/ppermute | solution.py:19
  428.6 24.9 %copy-start.96 = (s32[64]{0:T(128)S(1)}, s32[64]{0:T(128)}, u32[]{:S(2)}) copy-start(s32[64]{0:T(128)} %constant.312) | copy-start | bytes 772
  435.5 23.6 %copy-start.41 = (f32[2,1,3,3,256]{4,1,3,2,0:T(1,128)S(1)}, f32[2,1,3,3,256]{4,1,3,2,0:T(1,128)}, u32[]{:S(2)}) copy-start(f32[2,1,3,3,256]{4,1,3,2,0:T(1,128)} %get-tuple-element.164) | copy-start | bytes 55300
  440.4 37.2 %copy-start.95 = (s32[64]{0:T(128)S(1)}, s32[64]{0:T(128)}, u32[]{:S(2)}) copy-start(s32[64]{0:T(128)} %constant.306) | copy-start | bytes 772
  445.9 121.2 %collective-permute-start.2 = (f32[594,64]{1,0:T(8,128)}, f32[594,64]{1,0:T(8,128)}, u32[]{:S(2)}, u32[]{:S(2)}) collective-permute-start(f32[594,64]{1,0:T(8,128)} %pad_maximum_fusion.3), channel_id=1, source_target_pairs={{0,16},{16,0},{4,20},{20,4},{8,24},{24,8},{12,28},{28,12},{32,48},... | collective-permute-start | bytes 456200 | tf_op jit(solution)/shard_map/ppermute | solution.py:29
  460.4 28.6 %copy-start.42 = (f32[2,1,3,3,256]{4,1,3,2,0:T(1,128)S(1)}, f32[2,1,3,3,256]{4,1,3,2,0:T(1,128)}, u32[]{:S(2)}) copy-start(f32[2,1,3,3,256]{4,1,3,2,0:T(1,128)} %get-tuple-element.165) | copy-start | bytes 55300
  465.8 144.2 %collective-permute-start.1 = (f32[594,64]{1,0:T(8,128)}, f32[594,64]{1,0:T(8,128)}, u32[]{:S(2)}, u32[]{:S(2)}) collective-permute-start(f32[594,64]{1,0:T(8,128)} %pad_maximum_fusion.2), channel_id=1, source_target_pairs={{0,8},{8,0},{4,12},{12,4},{16,24},{24,16},{20,28},{28,20},{32,40},... | collective-permute-start | bytes 456200 | tf_op jit(solution)/shard_map/ppermute | solution.py:29
  481.8 14.0 %copy-start.44 = (f32[2,1,3,3,256]{4,1,3,2,0:T(1,128)S(1)}, f32[2,1,3,3,256]{4,1,3,2,0:T(1,128)}, u32[]{:S(2)}) copy-start(f32[2,1,3,3,256]{4,1,3,2,0:T(1,128)} %copy-done.43) | copy-start | bytes 55300
  492.1 152.4 %collective-permute-start = (f32[594,64]{1,0:T(8,128)}, f32[594,64]{1,0:T(8,128)}, u32[]{:S(2)}, u32[]{:S(2)}) collective-permute-start(f32[594,64]{1,0:T(8,128)} %pad_maximum_fusion.1), channel_id=1, source_target_pairs={{0,4},{4,0},{8,12},{12,8},{16,20},{20,16},{24,28},{28,24},{32,36},... | collective-permute-start | bytes 456200 | tf_op jit(solution)/shard_map/ppermute | solution.py:29
  502.2 9.0 %copy-start.80 = (f32[1,3,1,256]{3,0,2,1:T(1,128)S(1)}, f32[1,3,1,256]{3,0,2,1:T(1,128)}, u32[]{:S(2)}) copy-start(f32[1,3,1,256]{3,0,2,1:T(1,128)} %get-tuple-element.184) | copy-start | bytes 9220
  513.5 20.0 %copy-start.12 = (f32[2,4,3,12,192]{4,1,3,2,0:T(4,128)S(1)}, f32[2,4,3,12,192]{4,1,3,2,0:T(4,128)}, u32[]{:S(2)}) copy-start(f32[2,4,3,12,192]{4,1,3,2,0:T(4,128)} %get-tuple-element.50) | copy-start | bytes 663556
  513.5 20.0 %copy-start.93 = (pred[256]{0:T(512)(128)(4,1)S(1)}, pred[256]{0:T(512)(128)(4,1)}, u32[]{:S(2)}) copy-start(pred[256]{0:T(512)(128)(4,1)} %constant.106) | copy-start | bytes 772
  535.0 16.1 %copy-start.11 = (f32[2,4,3,12,192]{4,1,3,2,0:T(4,128)S(1)}, f32[2,4,3,12,192]{4,1,3,2,0:T(4,128)}, u32[]{:S(2)}) copy-start(f32[2,4,3,12,192]{4,1,3,2,0:T(4,128)} %get-tuple-element.49) | copy-start | bytes 663556
  535.0 16.1 %copy-start.85 = (pred[256]{0:T(512)(128)(4,1)S(1)}, pred[256]{0:T(512)(128)(4,1)}, u32[]{:S(2)}) copy-start(pred[256]{0:T(512)(128)(4,1)} %constant.107) | copy-start | bytes 772
  567.1 15.1 %copy-start.10 = (f32[2,4,3,12,240]{4,1,3,2,0:T(4,128)S(1)}, f32[2,4,3,12,240]{4,1,3,2,0:T(4,128)}, u32[]{:S(2)}) copy-start(f32[2,4,3,12,240]{4,1,3,2,0:T(4,128)} %get-tuple-element.57) | copy-start | bytes 829444
  567.1 15.1 %copy-start.84 = (pred[256]{0:T(512)(128)(4,1)S(1)}, pred[256]{0:T(512)(128)(4,1)}, u32[]{:S(2)}) copy-start(pred[256]{0:T(512)(128)(4,1)} %constant.105) | copy-start | bytes 772
  578.4 10.2 %copy-start.79 = (s32[1024]{0:T(1024)S(1)}, s32[1024]{0:T(1024)}, u32[]{:S(2)}) copy-start(s32[1024]{0:T(1024)} %get-tuple-element.201) | copy-start | bytes 12292
  594.3 13.4 %copy-start.9 = (f32[2,4,3,12,240]{4,1,3,2,0:T(4,128)S(1)}, f32[2,4,3,12,240]{4,1,3,2,0:T(4,128)}, u32[]{:S(2)}) copy-start(f32[2,4,3,12,240]{4,1,3,2,0:T(4,128)} %get-tuple-element.58) | copy-start | bytes 829444
  594.3 13.4 %copy-start.92 = (pred[256]{0:T(512)(128)(4,1)S(1)}, pred[256]{0:T(512)(128)(4,1)}, u32[]{:S(2)}) copy-start(pred[256]{0:T(512)(128)(4,1)} %constant.104) | copy-start | bytes 772
  620.5 8.8 %copy-start.94 = (pred[256]{0:T(512)(128)(4,1)S(1)}, pred[256]{0:T(512)(128)(4,1)}, u32[]{:S(2)}) copy-start(pred[256]{0:T(512)(128)(4,1)} %constant.102) | copy-start | bytes 772
  644.5 9.9 %copy-start.8 = (f32[2,4,3,12,255]{4,1,3,2,0:T(4,128)S(1)}, f32[2,4,3,12,255]{4,1,3,2,0:T(4,128)}, u32[]{:S(2)}) copy-start(f32[2,4,3,12,255]{4,1,3,2,0:T(4,128)} %get-tuple-element.75) | copy-start | bytes 881284
  644.5 9.9 %copy-start.83 = (pred[256]{0:T(512)(128)(4,1)S(1)}, pred[256]{0:T(512)(128)(4,1)}, u32[]{:S(2)}) copy-start(pred[256]{0:T(512)(128)(4,1)} %constant.101) | copy-start | bytes 772
  662.9 10.1 %copy-start.7 = (f32[2,4,3,12,255]{4,1,3,2,0:T(4,128)S(1)}, f32[2,4,3,12,255]{4,1,3,2,0:T(4,128)}, u32[]{:S(2)}) copy-start(f32[2,4,3,12,255]{4,1,3,2,0:T(4,128)} %get-tuple-element.76) | copy-start | bytes 881284
  662.9 10.1 %copy-start.25 = (f32[2,4,3,12,1]{4,1,3,2,0:T(4,128)S(1)}, f32[2,4,3,12,1]{4,1,3,2,0:T(4,128)}, u32[]{:S(2)}) copy-start(f32[2,4,3,12,1]{4,1,3,2,0:T(4,128)} %get-tuple-element.74) | copy-start | bytes 3460
  662.9 10.1 %copy-start.91 = (pred[256]{0:T(512)(128)(4,1)S(1)}, pred[256]{0:T(512)(128)(4,1)}, u32[]{:S(2)}) copy-start(pred[256]{0:T(512)(128)(4,1)} %constant.100) | copy-start | bytes 772
  (73 other events, 290.0 us)
where the time goes:
time: 686 us; the launch traced here: 677 us
  blocking collectives  382 us (56%)
  local copies, waits for them, and re-layouts  219 us (32%)
  other arithmetic  38.2 us (6%)
  starting transfers between devices  24.6 us (4%)
  matrix products  9.97 us (1%)
    psum x1, blocking collectives, body(): amplitudes = lax.psum(partial_amplitude, 'site')  305 us
    gather x20, local copies, waits for them, and re-layouts, join_face(): jnp.take(received_values, jnp.asarray(slots), axis=received_values.ndim - 1)  78.8 us
    unnamed x1, blocking collectives  65.2 us
    gather x23, local copies, waits for them, and re-layouts, face_of(): return jnp.take(field, jnp.asarray(chosen), axis=field.ndim - 1)  40.4 us
    unnamed x229, local copies, waits for them, and re-layouts  18.1 us
    mul x52, local copies, waits for them, and re-layouts, colour_dagger(): real_terms.append(link_real * spin_real + link_imag * spin_imag)  17.8 us
    ppermute x3, starting transfers between devices, partner(): return lax.ppermute(block, axis, route)  15.5 us
  transfers between devices with their start and end apart: 5, of which 0 were waited for; matrix products, arithmetic and copies ran while one was open for 30% of the time, Pallas kernels for 0%

commit v1 on v0

v1 whole, which is shorter than its diff:
```python
import functools

import jax
import jax.numpy as jnp
from jax import lax
from jax.experimental import pallas as pl
from jax.experimental.pallas import tpu as pltpu
from jax.sharding import PartitionSpec as P

MESH = pl.DeviceIdType.MESH
F32 = jnp.float32
BF16 = jnp.bfloat16

EDGE = 4
LS = 12
NV = 128
VOL = EDGE**4
NS = 4
FIFTH_MASS = 0.4
WALL_HEIGHT = 1.8
VMEM_LIMIT = 48 * 1024 * 1024


def dot_nt(left, right):
    return lax.dot_general(left, right, (((1,), (1,)), ((), ())), preferred_element_type=F32)


def dot_nn(left, right):
    return jnp.dot(left, right, preferred_element_type=F32)


def site_selector(direction, level):
    stride = EDGE**direction
    lane = lax.broadcasted_iota(jnp.int32, (VOL, 128), 0)
    col = lax.broadcasted_iota(jnp.int32, (VOL, 128), 1)
    cell = col & 63
    site = (cell & (stride - 1)) + level * stride + (cell // stride) * (stride * EDGE)
    match = lane == site
    low = jnp.where(match & (col < 64), 1.0, 0.0).astype(BF16)
    high = jnp.where(match & (col >= 64), 1.0, 0.0).astype(BF16)
    return low, high


def times_i(value):
    return (-value[1], value[0])


def neg(value):
    return (-value[0], -value[1])


def add(left, right):
    return (left[0] + right[0], left[1] + right[1])


def sub(left, right):
    return (left[0] - right[0], left[1] - right[1])


def spin_e(direction, first, second):
    if direction == 0:
        return times_i(second), times_i(first)
    if direction == 1:
        return second, neg(first)
    if direction == 2:
        return times_i(first), neg(times_i(second))
    return first, second


def spin_e_dagger(direction, first, second):
    if direction == 0:
        return neg(times_i(second)), neg(times_i(first))
    if direction == 1:
        return neg(second), first
    if direction == 2:
        return neg(times_i(first)), times_i(second)
    return first, second


def half_spinors(direction, load):
    minus = [None] * 6
    plus = [None] * 6
    for colour in range(3):
        lowers = spin_e(direction, load(6 + colour), load(9 + colour))
        for spin in range(2):
            upper = load(3 * spin + colour)
            minus[3 * spin + colour] = sub(upper, lowers[spin])
            plus[3 * spin + colour] = add(upper, lowers[spin])
    return minus, plus


def neighbours(block, blocks):
    ahead = []
    behind = []
    for direction in range(3):
        step = 1 << direction
        other = block + step - 2 * step * ((block // step) % 2)
        ahead.append(other)
        behind.append(other)
    ahead.append((block + 8) % blocks)
    behind.append((block + blocks - 8) % blocks)
    return ahead, behind


def guess_kernel(
    blocks,
    src_ref, basis_ref, comp_ref, eig_ref, links_ref,
    guess_out, fwd_out, bwd_out, rlinks_out,
    low_src, gathered, trans, parts, incoming, sums_t, sums_y,
    link_rows, link_in, fwd_send, bwd_send, fwd_in, bwd_in,
    gather_s, gather_r, parts_s, parts_r, t_s, t_r, y_s, y_r,
    link_s, link_r, fwd_s, fwd_r, bwd_s, bwd_r,
):
    block = lax.axis_index("site")
    mine = lax.axis_index("src")
    slices = blocks // 8
    time = block // 8
    place = block % 8
    ahead, behind = neighbours(block, blocks)

    def src_peer(step):
        return (block, (mine + step) % NS)

    def time_peer(step):
        return (((time + step) % slices) * 8 + place, mine)

    def place_peer(step):
        return (time * 8 + (place + step) % 8, mine)

    barrier = pltpu.get_barrier_semaphore()
    for count, peer in ((NS, src_peer), (slices, time_peer), (8, place_peer)):
        for step in range(1, count):
            pl.semaphore_signal(barrier, inc=1, device_id=peer(step), device_id_type=MESH)

    for a in range(12):
        for part in range(2):
            for half in range(2):
                rows = src_ref[pl.ds(24 * (part * 12 + a) + half, LS, stride=2), :]
                low_src[a, part * 16 : part * 16 + LS, half * 128 : half * 128 + 128] = rows
    product = jnp.zeros((32, 256), F32)
    for a in range(12):
        tile = basis_ref[:, a].reshape(2 * NV, VOL)
        product += dot_nt(low_src[a].astype(BF16), tile)
    gathered[0, 0] = (product[0:16, 0:128] + product[16:32, 128:256]).astype(BF16)
    gathered[0, 1] = (product[16:32, 0:128] - product[0:16, 128:256]).astype(BF16)

    for direction in range(4):
        for part in range(2):
            for row in range(3):
                for colour in range(3):
                    at = part * 9 + row * 3 + colour
                    link_rows[direction, at : at + 1, :] = links_ref[
                        part, row, colour, direction : direction + 1, :
                    ]

    pl.semaphore_wait(barrier, NS - 1 + slices - 1 + 7)

    gathers = []
    for step in range(1, NS):
        copy = pltpu.make_async_remote_copy(
            src_ref=gathered.at[0], dst_ref=gathered.at[step],
            send_sem=gather_s.at[step], recv_sem=gather_r.at[step],
            device_id=src_peer(step), device_id_type=MESH,
        )
        copy.start()
        gathers.append(copy)
    link_copies = []
    for direction in range(4):
        copy = pltpu.make_async_remote_copy(
            src_ref=link_rows.at[direction], dst_ref=link_in.at[direction],
            send_sem=link_s.at[direction], recv_sem=link_r.at[direction],
            device_id=(ahead[direction], mine), device_id_type=MESH,
        )
        copy.start()
        link_copies.append(copy)
    for copy in gathers:
        copy.wait()

    for step in range(NS):
        for part in range(2):
            trans[pl.ds(part * NS + step, 16, stride=8), :] = gathered[step, part].astype(F32)

    def table(pair):
        halves = [
            jnp.concatenate([comp_ref[part, 2 * pair], comp_ref[part, 2 * pair + 1]], axis=1)
            for part in range(2)
        ]
        return jnp.concatenate(halves, axis=0)

    summed = jnp.zeros((8, 256), F32)
    for pair in range(6):
        rows = jnp.concatenate(
            [trans[16 * pair : 16 * pair + 8, :], trans[16 * pair + 8 : 16 * pair + 16, :]], axis=1
        )
        summed += dot_nt(rows.astype(BF16), table(pair))
    upper_rows = lax.broadcasted_iota(jnp.int32, (8, 128), 0) < NS
    turned = pltpu.roll(summed[:, 128:256], NS, 0)
    amplitude = summed[:, 0:128] + jnp.where(upper_rows, turned, -turned)

    def exchange(slots, here, count, peer, send_sems, recv_sems):
        copies = []
        for step in range(1, count):
            copy = pltpu.make_async_remote_copy(
                src_ref=slots.at[here], dst_ref=slots.at[here],
                send_sem=send_sems.at[step], recv_sem=recv_sems.at[step],
                device_id=peer(step), device_id_type=MESH,
            )
            copy.start()
            copies.append(copy)
        for copy in copies:
            copy.wait()

    sums_t[pl.ds(time, 1)] = amplitude[None]
    exchange(sums_t, time, slices, time_peer, t_s, t_r)
    sums_y[pl.ds(place, 1)] = jnp.sum(sums_t[...], axis=0, keepdims=True)
    exchange(sums_y, place, 8, place_peer, y_s, y_r)
    amplitude = jnp.sum(sums_y[...], axis=0)

    weights = (amplitude / eig_ref[...]).astype(BF16).astype(F32)
    turned = pltpu.roll(weights, NS, 0)
    weights = jnp.concatenate([weights, jnp.where(upper_rows, -turned, turned)], axis=1).astype(BF16)
    for pair in range(6):
        out = dot_nn(weights, table(pair))
        trans[16 * pair : 16 * pair + 8, :] = out[:, 0:128]
        trans[16 * pair + 8 : 16 * pair + 16, :] = out[:, 128:256]
    for step in range(NS):
        for part in range(2):
            parts[step, part] = trans[pl.ds(part * NS + step, 16, stride=8), :]
    sends = []
    for step in range(1, NS):
        copy = pltpu.make_async_remote_copy(
            src_ref=parts.at[step], dst_ref=incoming.at[step],
            send_sem=parts_s.at[step], recv_sem=parts_r.at[step],
            device_id=src_peer(NS - step), device_id_type=MESH,
        )
        copy.start()
        sends.append(copy)
    for copy in sends:
        copy.wait()
    coarse = [
        (parts[0, part] + incoming[1, part] + incoming[2, part] + incoming[3, part]).astype(BF16)
        for part in range(2)
    ]
    left = jnp.concatenate(
        [
            jnp.concatenate([coarse[0], -coarse[1]], axis=1),
            jnp.concatenate([coarse[1], coarse[0]], axis=1),
        ],
        axis=0,
    )
    for a in range(12):
        guess_out[a] = dot_nn(left, basis_ref[:, a].reshape(2 * NV, VOL))

    def load(a):
        return guess_out[a, 0:16, :], guess_out[a, 16:32, :]

    copies = []
    for direction in (3, 2, 1, 0):
        minus, plus = half_spinors(direction, load)
        for values, level, send, land, peer, send_sems, recv_sems in (
            (minus, 0, fwd_send, fwd_in, behind, fwd_s, fwd_r),
            (plus, EDGE - 1, bwd_send, bwd_in, ahead, bwd_s, bwd_r),
        ):
            low, high = site_selector(direction, level)
            flat = [item.astype(BF16) for pair in values for item in pair]
            packed = dot_nn(jnp.concatenate(flat[:6], axis=0), low)
            packed += dot_nn(jnp.concatenate(flat[6:], axis=0), high)
            send[direction] = packed.astype(BF16)
            copy = pltpu.make_async_remote_copy(
                src_ref=send.at[direction], dst_ref=land.at[direction],
                send_sem=send_sems.at[direction], recv_sem=recv_sems.at[direction],
                device_id=(peer[direction], mine), device_id_type=MESH,
            )
            copy.start()
            copies.append(copy)
    for copy in link_copies:
        copy.wait()
    for copy in copies:
        copy.wait()
    fwd_out[...] = fwd_in[...]
    bwd_out[...] = bwd_in[...]
    rlinks_out[...] = link_in[...]


def dirac_kernel(
    src_ref, guess_ref, links_ref, rlinks_ref, fwd_ref, bwd_ref, out_ref,
    hop, halo_f, halo_b, link_rows,
):
    lane = lax.broadcasted_iota(jnp.int32, (24, VOL), 1)
    for direction in range(4):
        for part in range(2):
            for row in range(3):
                for colour in range(3):
                    at = part * 9 + row * 3 + colour
                    link_rows[direction, at : at + 1, :] = links_ref[
                        part, row, colour, direction : direction + 1, :
                    ]
    for direction in range(4):
        stride = EDGE**direction
        edge = (lane // stride) % EDGE == 0
        link_rows[4 + direction] = jnp.where(
            edge,
            pltpu.roll(rlinks_ref[direction], VOL - 3 * stride, 1),
            pltpu.roll(link_rows[direction], stride, 1),
        )
        for source, level, halo in ((fwd_ref, EDGE - 1, halo_f), (bwd_ref, 0, halo_b)):
            low, high = site_selector(direction, level)
            halo[direction, 0:96] = dot_nt(source[direction], low)
            halo[direction, 96:192] = dot_nt(source[direction], high)

    lane8 = lax.broadcasted_iota(jnp.int32, (8, VOL), 1)

    def group(index, carry):
        base = pl.multiple_of(index * 8, 8)

        def load(a):
            return guess_ref[a, pl.ds(base, 8), :], guess_ref[a, pl.ds(base + 16, 8), :]

        for direction in range(4):
            stride = EDGE**direction
            coord = (lane8 // stride) % EDGE
            minus, plus = half_spinors(direction, load)

            def shifted(values, halo, amount, edge):
                result = []
                for comp in range(6):
                    result.append(
                        tuple(
                            jnp.where(
                                coord == edge,
                                halo[direction, pl.ds(base + comp * 32 + 16 * part, 8), :],
                                pltpu.roll(values[comp][part], amount, 1),
                            )
                            for part in range(2)
                        )
                    )
                return result

            forward = shifted(minus, halo_f, VOL - stride, EDGE - 1)
            backward = shifted(plus, halo_b, stride, 0)

            def link(which, part, row, colour):
                at = part * 9 + row * 3 + colour
                return link_rows[which, at : at + 1, :]

            moved = [None] * 6
            back = [None] * 6
            for row in range(3):
                for spin in range(2):
                    real = imag = 0.0
                    for colour in range(3):
                        link_re = link(direction, 0, row, colour)
                        link_im = link(direction, 1, row, colour)
                        re, im = forward[3 * spin + colour]
                        real = real + (link_re * re - link_im * im)
                        imag = imag + (link_re * im + link_im * re)
                    moved[3 * spin + row] = (real, imag)
                    real = imag = 0.0
                    for colour in range(3):
                        link_re = link(4 + direction, 0, colour, row)
                        link_im = link(4 + direction, 1, colour, row)
                        re, im = backward[3 * spin + colour]
                        real = real + (link_re * re + link_im * im)
                        imag = imag + (link_re * im - link_im * re)
                    back[3 * spin + row] = (real, imag)
            for colour in range(3):
                first = sub(back[colour], moved[colour])
                second = sub(back[3 + colour], moved[3 + colour])
                lowers = spin_e_dagger(direction, first, second)
                totals = [
                    add(back[colour], moved[colour]),
                    add(back[3 + colour], moved[3 + colour]),
                    lowers[0],
                    lowers[1],
                ]
                for spin in range(4):
                    for part in range(2):
                        rows = pl.ds(base + 16 * part, 8)
                        value = totals[spin][part]
                        if direction == 0:
                            hop[3 * spin + colour, rows, :] = value
                        else:
                            hop[3 * spin + colour, rows, :] += value
        return carry

    lax.fori_loop(0, 2, group, 0)

    for a in range(12):
        for part in range(2):
            rows = slice(part * 16, part * 16 + LS)
            value = guess_ref[a, rows, :]
            if a < 6:
                fifth = jnp.concatenate([-FIFTH_MASS * value[LS - 1 : LS], value[0 : LS - 1]], axis=0)
            else:
                fifth = jnp.concatenate([value[1:LS], -FIFTH_MASS * value[0:1]], axis=0)
            applied = (5.0 - WALL_HEIGHT) * value - 0.5 * hop[a, rows, :] - fifth
            for half in range(2):
                at = pl.ds(24 * (part * 12 + a) + half, LS, stride=2)
                out_ref[at, :] = src_ref[at, :] - applied[:, half * 128 : half * 128 + 128]


def body(blocks, source, basis, compressed, eigenvalues, links):
    flat_source = source.reshape(2 * 12 * LS * 2, 128)
    table = jnp.transpose(compressed.reshape(2, 128, LS, NV), (0, 2, 1, 3))
    link_table = jnp.transpose(links, (0, 2, 3, 1, 4))
    eig = eigenvalues.reshape(1, 128)
    vmem = pl.BlockSpec(memory_space=pltpu.VMEM)
    dma = pltpu.SemaphoreType.DMA
    guess, fwd, bwd, rlinks = pl.pallas_call(
        functools.partial(guess_kernel, blocks),
        out_shape=(
            jax.ShapeDtypeStruct((12, 32, VOL), F32),
            jax.ShapeDtypeStruct((4, 96, 128), BF16),
            jax.ShapeDtypeStruct((4, 96, 128), BF16),
            jax.ShapeDtypeStruct((4, 24, VOL), F32),
        ),
        in_specs=[vmem] * 5,
        out_specs=(vmem,) * 4,
        scratch_shapes=[
            pltpu.VMEM((12, 32, VOL), F32),
            pltpu.VMEM((NS, 2, 16, 128), BF16),
            pltpu.VMEM((128, 128), F32),
            pltpu.VMEM((NS, 2, 16, 128), F32),
            pltpu.VMEM((NS, 2, 16, 128), F32),
            pltpu.VMEM((blocks // 8, 8, 128), F32),
            pltpu.VMEM((8, 8, 128), F32),
            pltpu.VMEM((4, 24, VOL), F32),
            pltpu.VMEM((4, 24, VOL), F32),
            pltpu.VMEM((4, 96, 128), BF16),
            pltpu.VMEM((4, 96, 128), BF16),
            pltpu.VMEM((4, 96, 128), BF16),
            pltpu.VMEM((4, 96, 128), BF16),
            dma((NS,)), dma((NS,)), dma((NS,)), dma((NS,)),
            dma((blocks // 8,)), dma((blocks // 8,)), dma((8,)), dma((8,)),
            dma((4,)), dma((4,)), dma((4,)), dma((4,)), dma((4,)), dma((4,)),
        ],
        compiler_params=pltpu.CompilerParams(
            collective_id=0, has_side_effects=True, vmem_limit_bytes=VMEM_LIMIT
        ),
        name="deflated_guess",
    )(flat_source, basis, table, eig, link_table)
    residual = pl.pallas_call(
        dirac_kernel,
        out_shape=jax.ShapeDtypeStruct((576, 128), F32),
        in_specs=[vmem] * 6,
        out_specs=vmem,
        scratch_shapes=[
            pltpu.VMEM((12, 32, VOL), F32),
            pltpu.VMEM((4, 192, VOL), F32),
            pltpu.VMEM((4, 192, VOL), F32),
            pltpu.VMEM((8, 24, VOL), F32),
        ],
        compiler_params=pltpu.CompilerParams(vmem_limit_bytes=VMEM_LIMIT),
        name="dirac",
    )(flat_source, guess, link_table, rlinks, fwd, bwd)
    return residual.reshape(source.shape)


def solution(mesh):
    in_specs = (
        P(None, None, "src", None, "site"),
        P(None, None, None, "site"),
        P(None, "src", "site", None, None),
        P("src"),
        P(None, None, None, None, "site"),
    )
    out_specs = P(None, None, "src", None, "site")
    step = functools.partial(body, mesh.shape["site"])
    return jax.shard_map(step, mesh=mesh, in_specs=in_specs, out_specs=out_specs, check_vma=False)
```

time: 686 us -> 48.2 us (0.07); the launches traced: 677 us -> 47.9 us
  blocking collectives: 382 us -> 0 us
  local copies, waits for them, and re-layouts: 219 us -> 5.04 us
  Pallas kernels: 0 us -> 42.9 us
  other arithmetic: 38.2 us -> 0 us
  starting transfers between devices: 24.6 us -> 0 us
  matrix products: 9.97 us -> 0 us
    psum x1 -> x0, blocking collectives: 305 us -> none  [body(): amplitudes = lax.psum(partial_amplitude, 'site')]
    gather x43 -> x0, local copies, waits for them, and re-layouts: 119 us -> none  [the longest x20 78.8 us: join_face(): jnp.take(received_values, jnp.asarray(slots), axis=received_values.ndim - 1)]
    unnamed x1 -> x0, blocking collectives: 65.2 us -> none
    pallas_call x0 -> x2, Pallas kernels: none -> 42.9 us  [the longest x1 40.2 us: body(): pl.pallas_call(functools.partial(guess_kernel, blocks), out_shape=(jax.Sh...]
    reshape x35 -> x0, local copies, waits for them, and re-layouts: 25.6 us -> none  [the longest x8 8.23 us: hop_direction(): back_in[:guess_rows].reshape(back_guess.shape)]
    ppermute x5 -> x0, starting transfers between devices: 24.6 us -> none  [the longest x3 15.5 us: partner(): return lax.ppermute(block, axis, route)]
    slice x34 -> x0, local copies, waits for them, and re-layouts: 23.7 us -> none  [the longest x10 5.67 us: join_face(): jnp.roll(field, stride, axis=field.ndim - 1)]
    mul x80 -> x0, local copies, waits for them, and re-layouts: 18 us -> none  [the longest x52 17.8 us: colour_dagger(): real_terms.append(link_real * spin_real + link_imag * spin_imag)]
  transfers between devices with their start and end apart: 5 -> 0, of which waited for: 0 -> 0; matrix products, arithmetic and copies ran while one was open for 30% -> 0% of each run, Pallas kernels for 0% -> 0%
where the time goes in v1:
time: 48.2 us; the launch traced here: 47.9 us
  Pallas kernels  42.9 us (89%)
  local copies, waits for them, and re-layouts  5.04 us (10%)
    pallas_call x1, Pallas kernels, body(): pl.pallas_call(functools.partial(guess_kernel, blocks), out_shape=(jax.Sh...  40.2 us
    unnamed x10, local copies, waits for them, and re-layouts  5.04 us
    pallas_call x1, Pallas kernels, body(): pl.pallas_call(dirac_kernel, out_shape=jax.ShapeDtypeStruct((576, 128), F...  2.62 us

profile of v1, /device:TPU:1, one launch (start us, length us, event | category | flops | bytes accessed | tf_op | source)
XLA Modules:
  0.0 47.9 jit_solution(17931837271639192289)
XLA Ops:
  0.0 0.0 copy-start
  0.0 1.4 %copy-done = bf16[2,12,128,256]{3,2,1,0:T(8,128)(2,1)S(1)} copy-done((bf16[2,12,128,256]{3,2,1,0:T(8,128)(2,1)S(1)}, bf16[2,12,128,256]{3,2,1,0:T(8,128)(2,1)}, u32[]{:S(2)}) %copy-start) | copy-done | bytes 1572888
  1.4 0.0 copy-start.1
  1.4 1.0 %copy-done.1 = f32[2,12,1,12,256]{4,2,3,1,0:T(1,128)S(1)} copy-done((f32[2,12,1,12,256]{4,2,3,1,0:T(1,128)S(1)}, f32[2,12,1,12,256]{4,2,3,1,0:T(1,128)}, u32[]{:S(2)}) %copy-start.1) | copy-done | bytes 294936
  2.4 0.0 copy-start.2
  2.4 1.1 %copy-done.2 = bf16[2,128,1,12,128]{4,1,3,2,0:T(8,128)(2,1)S(1)} copy-done((bf16[2,128,1,12,128]{4,1,3,2,0:T(8,128)(2,1)S(1)}, bf16[2,128,1,12,128]{4,1,3,2,0:T(8,128)(2,1)}, u32[]{:S(2)}) %copy-start.2) | copy-done | bytes 786456
  3.5 0.0 copy-start.3
  3.5 0.9 %copy-done.3 = f32[2,4,3,3,256]{4,1,3,2,0:T(4,128)S(1)} copy-done((f32[2,4,3,3,256]{4,1,3,2,0:T(4,128)S(1)}, f32[2,4,3,3,256]{4,1,3,2,0:T(4,128)}, u32[]{:S(2)}) %copy-start.3) | copy-done | bytes 73752
  4.4 0.0 copy-start.4
  4.4 0.7 %copy-done.4 = f32[128]{0:T(128)S(1)} copy-done((f32[128]{0:T(128)S(1)}, f32[128]{0:T(128)}, u32[]{:S(2)}) %copy-start.4) | copy-done | bytes 536
  5.0 40.2 %deflated_guess.1 = (f32[12,32,256]{2,1,0:T(8,128)S(1)}, bf16[4,96,128]{2,1,0:T(8,128)(2,1)S(1)}, bf16[4,96,128]{2,1,0:T(8,128)(2,1)S(1)}, f32[4,24,256]{2,1,0:T(8,128)S(1)}) custom-call(f32[576,128]{1,0:T(8,128)S(1)} %bitcast.7, bf16[2,12,128,256]{3,2,1,0:T(8,128)(2,1)S(1)} %copy-done, bf16[2,12,128,128]{3,2,1,0:T(8,128)(2,1)S(1)} %bitcast.9, ...), custom_call_target="tpu_custom_call" | custom-call | tf_op jit(solution)/shard_map/deflated_guess/pallas_call | solution.py:409
  45.3 2.6 %dirac.1 = f32[576,128]{1,0:T(8,128)} custom-call(f32[576,128]{1,0:T(8,128)S(1)} %bitcast.8, f32[12,32,256]{2,1,0:T(8,128)S(1)} %get-tuple-element.9.guess_ref, f32[2,3,3,4,256]{4,3,2,1,0:T(4,128)S(1)} %bitcast.11, f32[4,24,256]{2,1,0:T(8,128)S(1)} %get-tuple-element.10.rlinks_ref, bf16[4,96,128]{2,1,0:T(8,128)(2,1)S(1)} %get-tuple-element.11.fwd_ref, ...), custom_call_target="tpu_custom_call" | custom-call | tf_op jit(solution)/shard_map/dirac/pallas_call | solution.py:442
Async XLA Ops:
  0.0 1.4 %copy-start = (bf16[2,12,128,256]{3,2,1,0:T(8,128)(2,1)S(1)}, bf16[2,12,128,256]{3,2,1,0:T(8,128)(2,1)}, u32[]{:S(2)}) copy-start(bf16[2,12,128,256]{3,2,1,0:T(8,128)(2,1)} %basis_ref.1) | copy-start | bytes 4718596
  1.4 1.0 %copy-start.1 = (f32[2,12,1,12,256]{4,2,3,1,0:T(1,128)S(1)}, f32[2,12,1,12,256]{4,2,3,1,0:T(1,128)}, u32[]{:S(2)}) copy-start(f32[2,12,1,12,256]{4,2,3,1,0:T(1,128)} %param.5) | copy-start | bytes 884740
  2.4 1.1 %copy-start.2 = (bf16[2,128,1,12,128]{4,1,3,2,0:T(8,128)(2,1)S(1)}, bf16[2,128,1,12,128]{4,1,3,2,0:T(8,128)(2,1)}, u32[]{:S(2)}) copy-start(bf16[2,128,1,12,128]{4,1,3,2,0:T(8,128)(2,1)} %param.7) | copy-start | bytes 2359300
  3.5 0.9 %copy-start.3 = (f32[2,4,3,3,256]{4,1,3,2,0:T(4,128)S(1)}, f32[2,4,3,3,256]{4,1,3,2,0:T(4,128)}, u32[]{:S(2)}) copy-start(f32[2,4,3,3,256]{4,1,3,2,0:T(4,128)} %param.9) | copy-start | bytes 221188
  4.4 0.7 %copy-start.4 = (f32[128]{0:T(128)S(1)}, f32[128]{0:T(128)}, u32[]{:S(2)}) copy-start(f32[128]{0:T(128)} %param.8) | copy-start | bytes 1540

commit v2 on v1

v2 whole, which is shorter than its diff:
```python
import functools

import jax
import jax.numpy as jnp
from jax import lax
from jax.experimental import pallas as pl
from jax.experimental.pallas import tpu as pltpu
from jax.sharding import PartitionSpec as P

MESH = pl.DeviceIdType.MESH
F32 = jnp.float32
BF16 = jnp.bfloat16

EDGE = 4
LS = 12
NV = 128
VOL = EDGE**4
NS = 4
FIFTH_MASS = 0.4
WALL_HEIGHT = 1.8
VMEM_LIMIT = 64 * 1024 * 1024


def dot_nt(left, right):
    return lax.dot_general(left, right, (((1,), (1,)), ((), ())), preferred_element_type=F32)


def dot_nn(left, right):
    return jnp.dot(left, right, preferred_element_type=F32)


def site_selector(direction, level):
    stride = EDGE**direction
    lane = lax.broadcasted_iota(jnp.int32, (VOL, 128), 0)
    col = lax.broadcasted_iota(jnp.int32, (VOL, 128), 1)
    cell = col & 63
    site = (cell & (stride - 1)) + level * stride + (cell // stride) * (stride * EDGE)
    match = lane == site
    low = jnp.where(match & (col < 64), 1.0, 0.0).astype(BF16)
    high = jnp.where(match & (col >= 64), 1.0, 0.0).astype(BF16)
    return low, high


def times_i(value):
    return (-value[1], value[0])


def neg(value):
    return (-value[0], -value[1])


def add(left, right):
    return (left[0] + right[0], left[1] + right[1])


def sub(left, right):
    return (left[0] - right[0], left[1] - right[1])


def spin_e(direction, first, second):
    if direction == 0:
        return times_i(second), times_i(first)
    if direction == 1:
        return second, neg(first)
    if direction == 2:
        return times_i(first), neg(times_i(second))
    return first, second


def spin_e_dagger(direction, first, second):
    if direction == 0:
        return neg(times_i(second)), neg(times_i(first))
    if direction == 1:
        return neg(second), first
    if direction == 2:
        return neg(times_i(first)), times_i(second)
    return first, second


def half_spinors(direction, load):
    minus = [None] * 6
    plus = [None] * 6
    for colour in range(3):
        lowers = spin_e(direction, load(6 + colour), load(9 + colour))
        for spin in range(2):
            upper = load(3 * spin + colour)
            minus[3 * spin + colour] = sub(upper, lowers[spin])
            plus[3 * spin + colour] = add(upper, lowers[spin])
    return minus, plus


def neighbours(block, blocks):
    ahead = []
    behind = []
    for direction in range(3):
        step = 1 << direction
        other = block + step - 2 * step * ((block // step) % 2)
        ahead.append(other)
        behind.append(other)
    ahead.append((block + 8) % blocks)
    behind.append((block + blocks - 8) % blocks)
    return ahead, behind


def fused_kernel(
    blocks,
    src_hbm, basis_hbm, comp_hbm, eig_hbm, links_hbm,
    out_ref,
    src_ref, basis_ref, comp_ref, eig_ref, links_ref,
    low_src, gathered, trans, parts, incoming, sums_t, sums_y,
    link_rows, link_in, link_back, selectors, guess, total, halo_f, halo_b,
    fwd_send, bwd_send, fwd_in, bwd_in,
    load_s, gather_s, gather_r, parts_s, parts_r, t_s, t_r, y_s, y_r,
    link_s, link_r, fwd_s, fwd_r, bwd_s, bwd_r,
):
    block = lax.axis_index("site")
    mine = lax.axis_index("src")
    slices = blocks // 8
    time = block // 8
    place = block % 8
    ahead, behind = neighbours(block, blocks)

    def src_peer(step):
        return (block, (mine + step) % NS)

    def time_peer(step):
        return (((time + step) % slices) * 8 + place, mine)

    def place_peer(step):
        return (time * 8 + (place + step) % 8, mine)

    loads = []
    for index, (far, near) in enumerate(
        (
            (src_hbm, src_ref), (basis_hbm, basis_ref), (links_hbm, links_ref),
            (comp_hbm, comp_ref), (eig_hbm, eig_ref),
        )
    ):
        copy = pltpu.make_async_copy(far, near, load_s.at[index])
        copy.start()
        loads.append(copy)

    barrier = pltpu.get_barrier_semaphore()
    for count, peer in ((NS, src_peer), (slices, time_peer), (8, place_peer)):
        for step in range(1, count):
            pl.semaphore_signal(barrier, inc=1, device_id=peer(step), device_id_type=MESH)

    loads[0].wait()
    for a in range(12):
        for part in range(2):
            for half in range(2):
                rows = src_ref[pl.ds(24 * (part * 12 + a) + half, LS, stride=2), :]
                low_src[a, part * 16 : part * 16 + LS, half * 128 : half * 128 + 128] = rows
    loads[1].wait()
    product = jnp.zeros((32, 256), F32)
    for a in range(12):
        tile = basis_ref[:, a].reshape(2 * NV, VOL)
        product += dot_nt(low_src[a].astype(BF16), tile)
    gathered[0, 0] = (product[0:16, 0:128] + product[16:32, 128:256]).astype(BF16)
    gathered[0, 1] = (product[16:32, 0:128] - product[0:16, 128:256]).astype(BF16)

    pl.semaphore_wait(barrier, NS - 1 + slices - 1 + 7)

    sent = []

    def send(source, target, send_sem, recv_sem, peer):
        copy = pltpu.make_async_remote_copy(
            src_ref=source, dst_ref=target, send_sem=send_sem, recv_sem=recv_sem,
            device_id=peer, device_id_type=MESH,
        )
        copy.start()
        sent.append(copy)
        return copy

    gathers = [
        send(gathered.at[0], gathered.at[step], gather_s.at[step], gather_r.at[step], src_peer(step))
        for step in range(1, NS)
    ]

    loads[2].wait()
    for direction in range(4):
        for part in range(2):
            for row in range(3):
                for colour in range(3):
                    at = part * 9 + row * 3 + colour
                    link_rows[direction, at : at + 1, :] = (
                        0.5 * links_ref[part, row, colour, direction : direction + 1, :]
                    )
    link_copies = [
        send(
            link_rows.at[direction], link_in.at[direction],
            link_s.at[direction], link_r.at[direction], (ahead[direction], mine),
        )
        for direction in range(4)
    ]
    loads[3].wait()
    loads[4].wait()
    for copy in gathers:
        copy.wait_recv()

    for step in range(NS):
        for part in range(2):
            trans[pl.ds(part * NS + step, 16, stride=8), :] = gathered[step, part].astype(F32)

    def table(pair):
        halves = [
            jnp.concatenate([comp_ref[part, 2 * pair], comp_ref[part, 2 * pair + 1]], axis=1)
            for part in range(2)
        ]
        return jnp.concatenate(halves, axis=0)

    summed = jnp.zeros((8, 256), F32)
    for pair in range(6):
        rows = jnp.concatenate(
            [trans[16 * pair : 16 * pair + 8, :], trans[16 * pair + 8 : 16 * pair + 16, :]], axis=1
        )
        summed += dot_nt(rows.astype(BF16), table(pair))
    upper_rows = lax.broadcasted_iota(jnp.int32, (8, 128), 0) < NS
    turned = pltpu.roll(summed[:, 128:256], NS, 0)
    amplitude = summed[:, 0:128] + jnp.where(upper_rows, turned, -turned)

    def exchange(slots, here, count, peer, send_sems, recv_sems):
        return [
            send(slots.at[here], slots.at[here], send_sems.at[step], recv_sems.at[step], peer(step))
            for step in range(1, count)
        ]

    sums_t[pl.ds(time, 1)] = amplitude[None]
    copies = exchange(sums_t, time, slices, time_peer, t_s, t_r)
    for direction in range(4):
        for index, level in enumerate((0, EDGE - 1)):
            low, high = site_selector(direction, level)
            selectors[direction, index, 0] = low
            selectors[direction, index, 1] = high
    for copy in copies:
        copy.wait_recv()
    sums_y[pl.ds(place, 1)] = jnp.sum(sums_t[...], axis=0, keepdims=True)
    copies = exchange(sums_y, place, 8, place_peer, y_s, y_r)
    for copy in link_copies:
        copy.wait_recv()
    lane = lax.broadcasted_iota(jnp.int32, (24, VOL), 1)
    for direction in range(4):
        stride = EDGE**direction
        link_back[direction] = jnp.where(
            (lane // stride) % EDGE == 0,
            pltpu.roll(link_in[direction], VOL - 3 * stride, 1),
            pltpu.roll(link_rows[direction], stride, 1),
        )
    for copy in copies:
        copy.wait_recv()
    amplitude = jnp.sum(sums_y[...], axis=0)

    weights = (amplitude / eig_ref[...]).astype(BF16).astype(F32)
    turned = pltpu.roll(weights, NS, 0)
    weights = jnp.concatenate([weights, jnp.where(upper_rows, -turned, turned)], axis=1).astype(BF16)
    for pair in range(6):
        out = dot_nn(weights, table(pair))
        trans[16 * pair : 16 * pair + 8, :] = out[:, 0:128]
        trans[16 * pair + 8 : 16 * pair + 16, :] = out[:, 128:256]
    for step in range(NS):
        for part in range(2):
            parts[step, part] = trans[pl.ds(part * NS + step, 16, stride=8), :]
    copies = [
        send(parts.at[step], incoming.at[step], parts_s.at[step], parts_r.at[step], src_peer(NS - step))
        for step in range(1, NS)
    ]
    for copy in copies:
        copy.wait_recv()
    coarse = [
        (parts[0, part] + incoming[1, part] + incoming[2, part] + incoming[3, part]).astype(BF16)
        for part in range(2)
    ]
    left = jnp.concatenate(
        [
            jnp.concatenate([coarse[0], -coarse[1]], axis=1),
            jnp.concatenate([coarse[1], coarse[0]], axis=1),
        ],
        axis=0,
    )
    for a in range(12):
        guess[a] = dot_nn(left, basis_ref[:, a].reshape(2 * NV, VOL))

    def load(a):
        return guess[a, 0:16, :], guess[a, 16:32, :]

    order = (2, 3, 1, 0)
    faces = {}
    for direction in order:
        minus, plus = half_spinors(direction, load)
        faces[direction] = []
        for values, index, out, land, peer, send_sems, recv_sems in (
            (minus, 0, fwd_send, fwd_in, behind, fwd_s, fwd_r),
            (plus, 1, bwd_send, bwd_in, ahead, bwd_s, bwd_r),
        ):
            flat = [item.astype(BF16) for pair in values for item in pair]
            packed = dot_nn(jnp.concatenate(flat[:6], axis=0), selectors[direction, index, 0])
            packed += dot_nn(jnp.concatenate(flat[6:], axis=0), selectors[direction, index, 1])
            out[direction] = packed.astype(BF16)
            faces[direction].append(
                send(
                    out.at[direction], land.at[direction],
                    send_sems.at[direction], recv_sems.at[direction], (peer[direction], mine),
                )
            )

    for a in range(12):
        for part in range(2):
            rows = slice(part * 16, part * 16 + LS)
            value = guess[a, rows, :]
            if a < 6:
                fifth = jnp.concatenate([-FIFTH_MASS * value[LS - 1 : LS], value[0 : LS - 1]], axis=0)
            else:
                fifth = jnp.concatenate([value[1:LS], -FIFTH_MASS * value[0:1]], axis=0)
            total[a, rows, :] = low_src[a, rows, :] - (5.0 - WALL_HEIGHT) * value + fifth

    lane8 = lax.broadcasted_iota(jnp.int32, (8, VOL), 1)
    for direction in reversed(order):
        for copy, source, index, halo in zip(
            faces[direction], (fwd_in, bwd_in), (1, 0), (halo_f, halo_b), strict=True
        ):
            copy.wait_recv()
            halo[0:96] = dot_nt(source[direction], selectors[direction, index, 0])
            halo[96:192] = dot_nt(source[direction], selectors[direction, index, 1])

        def group(which, carry, direction=direction):
            base = pl.multiple_of(which * 8, 8)
            stride = EDGE**direction
            coord = (lane8 // stride) % EDGE

            def rows_of(a):
                return guess[a, pl.ds(base, 8), :], guess[a, pl.ds(base + 16, 8), :]

            minus, plus = half_spinors(direction, rows_of)

            def shifted(values, halo, amount, edge):
                return [
                    tuple(
                        jnp.where(
                            coord == edge,
                            halo[pl.ds(base + comp * 32 + 16 * part, 8), :],
                            pltpu.roll(values[comp][part], amount, 1),
                        )
                        for part in range(2)
                    )
                    for comp in range(6)
                ]

            forward = shifted(minus, halo_f, VOL - stride, EDGE - 1)
            backward = shifted(plus, halo_b, stride, 0)

            def link(rows, part, row, colour):
                at = part * 9 + row * 3 + colour
                return rows[direction, at : at + 1, :]

            moved = [None] * 6
            back = [None] * 6
            for row in range(3):
                for spin in range(2):
                    real = imag = 0.0
                    for colour in range(3):
                        link_re = link(link_rows, 0, row, colour)
                        link_im = link(link_rows, 1, row, colour)
                        re, im = forward[3 * spin + colour]
                        real = real + (link_re * re - link_im * im)
                        imag = imag + (link_re * im + link_im * re)
                    moved[3 * spin + row] = (real, imag)
                    real = imag = 0.0
                    for colour in range(3):
                        link_re = link(link_back, 0, colour, row)
                        link_im = link(link_back, 1, colour, row)
                        re, im = backward[3 * spin + colour]
                        real = real + (link_re * re + link_im * im)
                        imag = imag + (link_re * im - link_im * re)
                    back[3 * spin + row] = (real, imag)
            for colour in range(3):
                first = sub(back[colour], moved[colour])
                second = sub(back[3 + colour], moved[3 + colour])
                lowers = spin_e_dagger(direction, first, second)
                totals = [
                    add(back[colour], moved[colour]),
                    add(back[3 + colour], moved[3 + colour]),
                    lowers[0],
                    lowers[1],
                ]
                for spin in range(4):
                    for part in range(2):
                        rows = pl.ds(base + 16 * part, 8)
                        total[3 * spin + colour, rows, :] += totals[spin][part]
            return carry

        lax.fori_loop(0, 2, group, 0)

    for a in range(12):
        for part in range(2):
            for half in range(2):
                out_ref[pl.ds(24 * (part * 12 + a) + half, LS, stride=2), :] = total[
                    a, part * 16 : part * 16 + LS, half * 128 : half * 128 + 128
                ]
    for copy in sent:
        copy.wait_send()


def body(blocks, source, basis, compressed, eigenvalues, links):
    flat_source = source.reshape(2 * 12 * LS * 2, 128)
    table = jnp.transpose(compressed.reshape(2, 128, LS, NV), (0, 2, 1, 3))
    link_table = jnp.transpose(links, (0, 2, 3, 1, 4))
    eig = eigenvalues.reshape(1, 128)
    dma = pltpu.SemaphoreType.DMA
    residual = pl.pallas_call(
        functools.partial(fused_kernel, blocks),
        out_shape=jax.ShapeDtypeStruct((576, 128), F32),
        in_specs=[pl.BlockSpec(memory_space=pltpu.HBM)] * 5,
        out_specs=pl.BlockSpec(memory_space=pltpu.VMEM),
        scratch_shapes=[
            pltpu.VMEM((576, 128), F32),
            pltpu.VMEM((2, 12, NV, VOL), BF16),
            pltpu.VMEM((2, LS, 128, NV), BF16),
            pltpu.VMEM((1, 128), F32),
            pltpu.VMEM((2, 3, 3, 4, VOL), F32),
            pltpu.VMEM((12, 32, VOL), F32),
            pltpu.VMEM((NS, 2, 16, 128), BF16),
            pltpu.VMEM((128, 128), F32),
            pltpu.VMEM((NS, 2, 16, 128), F32),
            pltpu.VMEM((NS, 2, 16, 128), F32),
            pltpu.VMEM((blocks // 8, 8, 128), F32),
            pltpu.VMEM((8, 8, 128), F32),
            pltpu.VMEM((4, 24, VOL), F32),
            pltpu.VMEM((4, 24, VOL), F32),
            pltpu.VMEM((4, 24, VOL), F32),
            pltpu.VMEM((4, 2, 2, VOL, 128), BF16),
            pltpu.VMEM((12, 32, VOL), F32),
            pltpu.VMEM((12, 32, VOL), F32),
            pltpu.VMEM((192, VOL), F32),
            pltpu.VMEM((192, VOL), F32),
            pltpu.VMEM((4, 96, 128), BF16),
            pltpu.VMEM((4, 96, 128), BF16),
            pltpu.VMEM((4, 96, 128), BF16),
            pltpu.VMEM((4, 96, 128), BF16),
            dma((5,)),
            dma((NS,)), dma((NS,)), dma((NS,)), dma((NS,)),
            dma((blocks // 8,)), dma((blocks // 8,)), dma((8,)), dma((8,)),
            dma((4,)), dma((4,)), dma((4,)), dma((4,)), dma((4,)), dma((4,)),
        ],
        compiler_params=pltpu.CompilerParams(
            collective_id=0, has_side_effects=True, vmem_limit_bytes=VMEM_LIMIT
        ),
        name="deflated_residual",
    )(flat_source, basis, table, eig, link_table)
    return residual.reshape(source.shape)


def solution(mesh):
    in_specs = (
        P(None, None, "src", None, "site"),
        P(None, None, None, "site"),
        P(None, "src", "site", None, None),
        P("src"),
        P(None, None, None, None, "site"),
    )
    out_specs = P(None, None, "src", None, "site")
    step = functools.partial(body, mesh.shape["site"])
    return jax.shard_map(step, mesh=mesh, in_specs=in_specs, out_specs=out_specs, check_vma=False)
```

time: 48.2 us -> 45.1 us (0.936)
  local copies, waits for them, and re-layouts: 5.04 us -> 1.88 us
    unnamed x10 -> x1, local copies, waits for them, and re-layouts: 5.04 us -> 1.88 us
    pallas_call x2 -> x1, Pallas kernels: 42.9 us -> 43 us  [body(): pl.pallas_call(functools.partial(fused_kernel, blocks), out_shape=jax.Sha...]
where the time goes in v2:
time: 45.1 us; the launch traced here: 44.9 us
  Pallas kernels  43 us (95%)
  local copies, waits for them, and re-layouts  1.88 us (4%)
    pallas_call x1, Pallas kernels, body(): pl.pallas_call(functools.partial(fused_kernel, blocks), out_shape=jax.Sha...  43 us
    unnamed x1, local copies, waits for them, and re-layouts  1.88 us

profile of v2, /device:TPU:1, one launch (start us, length us, event | category | flops | bytes accessed | tf_op | source)
XLA Modules:
  0.0 44.9 jit_solution(9947003972557986554)
XLA Ops:
  0.0 43.0 %deflated_residual.1 = f32[576,128]{1,0:T(8,128)} custom-call(f32[576,128]{1,0:T(8,128)} %bitcast.9, bf16[2,12,128,256]{3,2,1,0:T(8,128)(2,1)} %basis_hbm.1, bf16[2,12,128,128]{3,2,1,0:T(8,128)(2,1)} %bitcast.8, f32[1,128]{1,0:T(1,128)} %bitcast.11, f32[2,3,3,4,256]{4,3,2,1,0:T(4,128)} %bitcast.10), custom_call_target="tpu_custom_call" | custom-call | tf_op jit(solution)/shard_map/deflated_residual/pallas_call | solution.py:409
  43.0 1.9 %copy.9 = f32[2,12,1,12,256]{4,2,3,1,0:T(1,128)} copy(f32[2,12,1,12,256]{4,2,3,1,0:T(1,128)} %bitcast.7) | data formatting | bytes 589824
